TPU v7x, 32 devices: a whole 2x2x4 slice. The times are simulated.
32 devices in a mesh: img: 16 (over z, x, core), row: 2 (over y).
Axes of the slice: x: 2, y: 2, z: 4, core: 2. Of those that a mesh axis runs over, the one named last changes fastest.
Arguments:
- llm_hidden: bfloat16 [8192, 6656], P('img', 'row'), may hold values from -96 to 96
- slot_start: int32 [16], P('img'), may hold values from 0 to 448
- image_group: int32 [16], replicated, may hold values from 0 to 15, each once
- timesteps: int32 [16], P('img'), may hold values from 0 to 999
- latents: float32 [16, 4, 16, 128], P('img', None, 'row'), may hold values from -6 to 6
- noise: float32 [16, 4, 16, 128], P('img', None, 'row'), may hold values from -6 to 6
- kv_weight: bfloat16 [6656, 640], P('row'), may hold values from -0.078125 to 0.078125
- in_weight: bfloat16 [3, 3, 320, 4], replicated, may hold values from -1 to 1
- res_weight: bfloat16 [3, 3, 320, 320], replicated, may hold values from -0.109375 to 0.109375
- query_weight: bfloat16 [320, 320], replicated, may hold values from -0.3125 to 0.3125
- out_weight: bfloat16 [320, 320], replicated, may hold values from -0.3125 to 0.3125
- cotangent: bfloat16 [16, 320, 16, 128], P('img', None, 'row'), may hold values from -6 to 6
Outputs:
- block_out: bfloat16 [16, 320, 16, 128], P('img', None, 'row')
- grad_hidden: bfloat16 [8192, 6656], P('img', 'row')
- grad_kv_weight: bfloat16 [6656, 640], P('row')
- grad_res_weight: bfloat16 [3, 3, 320, 320], replicated
- grad_query_weight: bfloat16 [320, 320], replicated
- grad_out_weight: bfloat16 [320, 320], replicated
Inputs may be any that keep to these rules, and one draw needn't show every extreme that they name: `slot_start`: each image's 64 condition rows lie inside its own sequence of 512 tokens. `image_group`: every group denoises exactly one image.
All inputs are finite; a program needn't handle non-finite values.
Results may differ from a plain program's by a relative error of at most 0.035.
The roundings to bfloat16 on the way count: a program that leaves them out, or rounds other values in their place, can miss the bound.
Values may be sent and summed in bfloat16 or wider, within the bound.
No kernel may reach another device: no remote copies, remote signals or barrier semaphores. Data moves between devices by JAX's collectives and lax.ppermute only.
A program may use at most 128 MiB of HBM per device.

v0:
```python
import math
import jax
import jax.numpy as jnp
from jax import lax
from jax.sharding import PartitionSpec as P

HEAD_DIM = 64
SLOTS = 64


def extended(cells, sides, width):
    for axis, dim in sides:
        count = lax.axis_size(axis)
        ends = count - 1
        head = lax.slice_in_dim(cells, 0, width, axis=dim)
        tail = lax.slice_in_dim(cells, cells.shape[dim] - width, cells.shape[dim], axis=dim)
        cells = jnp.concatenate(
            [
                lax.ppermute(tail, axis, [(i, (i + 1) % count) for i in range(ends)]),
                cells,
                lax.ppermute(head, axis, [((i + 1) % count, i) for i in range(ends)]),
            ],
            axis=dim,
        )
    return cells


def weighted_product(form, left, right):
    return jnp.einsum(form, left, right, preferred_element_type=jnp.float32)


def noise_levels():
    plan = jnp.linspace(0.00085**0.5, 0.012**0.5, 1000, dtype=jnp.float32) ** 2
    return jnp.exp(jnp.cumsum(jnp.log(1.0 - plan)))


def noisy_input(latent, noise_one, timestep):
    levels = noise_levels()
    picked = jnp.sum(jnp.where(jnp.arange(levels.shape[0]) == timestep, levels, 0.0))
    return (jnp.sqrt(picked) * latent + jnp.sqrt(1.0 - picked) * noise_one).astype(jnp.bfloat16)


def time_shift(timestep, channel_total):
    half_count = channel_total // 2
    frequency = jnp.exp(-math.log(10000.0) * jnp.arange(half_count, dtype=jnp.float32) / half_count)
    angles = timestep.astype(jnp.float32) * frequency
    return jnp.concatenate([jnp.cos(angles), jnp.sin(angles)])


def pad_columns(field):
    return jnp.pad(field, ((0, 0), (0, 0), (1, 1)))


def convolve(padded, weight, row_count, col_count):
    running = jnp.zeros((weight.shape[2], row_count * col_count), jnp.float32)
    for row_tap in range(3):
        for col_tap in range(3):
            window = padded[
                :, row_tap : row_tap + row_count, col_tap : col_tap + col_count
            ].reshape(padded.shape[0], row_count * col_count)
            running = running + jnp.dot(
                weight[row_tap, col_tap], window, preferred_element_type=jnp.float32
            )
    return running


def filter_grad(padded, upstream, row_count, col_count):
    tap_list = []
    for row_tap in range(3):
        for col_tap in range(3):
            window = padded[
                :, row_tap : row_tap + row_count, col_tap : col_tap + col_count
            ].reshape(padded.shape[0], row_count * col_count)
            tap_list.append(
                lax.dot_general(
                    upstream, window, (((1,), (1,)), ((), ())), preferred_element_type=jnp.float32
                )
            )
    return jnp.stack(tap_list).reshape(3, 3, upstream.shape[0], padded.shape[0])


def block_pass(
    noisy, timestep, group_kv, upstream, in_weight, res_weight, query_weight, out_weight
):
    channel_total = in_weight.shape[2]
    row_count, col_count = (noisy.shape[1], noisy.shape[2])
    latent_cell_count = row_count * col_count
    condition_slot_count = group_kv.shape[0]
    head_count = channel_total // HEAD_DIM
    logit_scale = HEAD_DIM ** (-0.5)
    noisy_pad = pad_columns(extended(noisy, (("row", 1),), 1))
    first = convolve(noisy_pad, in_weight, row_count, col_count)
    hidden_act = jax.nn.silu(first + time_shift(timestep, channel_total)[:, None]).astype(
        jnp.bfloat16
    )
    act_pad = pad_columns(
        extended(hidden_act.reshape(channel_total, row_count, col_count), (("row", 1),), 1)
    )
    residual = (first + convolve(act_pad, res_weight, row_count, col_count)).astype(jnp.bfloat16)
    query = jnp.dot(query_weight, residual, preferred_element_type=jnp.float32).astype(jnp.bfloat16)
    query_per_head = query.reshape(head_count, HEAD_DIM, latent_cell_count)
    key_matrix = group_kv[:, :channel_total].reshape(condition_slot_count, head_count, HEAD_DIM)
    value_matrix = group_kv[:, channel_total:].reshape(condition_slot_count, head_count, HEAD_DIM)
    score_matrix = weighted_product("isf,tis->itf", query_per_head, key_matrix) * logit_scale
    softmax_full = jax.nn.softmax(score_matrix, axis=1)
    softmax_reduced_precision = softmax_full.astype(jnp.bfloat16)
    attention_output = (
        weighted_product("cuo,ucb->cbo", softmax_reduced_precision, value_matrix)
        .astype(jnp.bfloat16)
        .reshape(channel_total, latent_cell_count)
    )
    block_out = (
        residual.astype(jnp.float32)
        + jnp.dot(out_weight, attention_output, preferred_element_type=jnp.float32)
    ).astype(jnp.bfloat16)
    upstream = upstream.reshape(channel_total, latent_cell_count)
    out_grad = lax.dot_general(
        upstream, attention_output, (((1,), (1,)), ((), ())), preferred_element_type=jnp.float32
    )
    grad_att = lax.dot_general(
        out_weight, upstream, (((0,), (0,)), ((), ())), preferred_element_type=jnp.float32
    ).astype(jnp.bfloat16)
    head_gradient = grad_att.reshape(head_count, HEAD_DIM, latent_cell_count)
    probability_gradient = weighted_product("isf,tis->itf", head_gradient, value_matrix)
    score_gradient = (
        logit_scale
        * softmax_full
        * (
            probability_gradient
            - jnp.sum(softmax_full * probability_gradient, axis=1, keepdims=True)
        )
    ).astype(jnp.bfloat16)
    query_gradient = (
        weighted_product("cuo,ucb->cbo", score_gradient, key_matrix)
        .astype(jnp.bfloat16)
        .reshape(channel_total, latent_cell_count)
    )
    key_gradient = weighted_product("exv,ewv->xew", score_gradient, query_per_head).reshape(
        condition_slot_count, channel_total
    )
    value_gradient = weighted_product(
        "exv,ewv->xew", softmax_reduced_precision, head_gradient
    ).reshape(condition_slot_count, channel_total)
    grad_kv = jnp.concatenate([key_gradient, value_gradient], axis=1)
    query_grad = lax.dot_general(
        query_gradient, residual, (((1,), (1,)), ((), ())), preferred_element_type=jnp.float32
    )
    grad_resid = (
        upstream.astype(jnp.float32)
        + lax.dot_general(
            query_weight,
            query_gradient,
            (((0,), (0,)), ((), ())),
            preferred_element_type=jnp.float32,
        )
    ).astype(jnp.bfloat16)
    res_grad = filter_grad(act_pad, grad_resid, row_count, col_count)
    return (
        block_out.reshape(channel_total, row_count, col_count),
        grad_kv,
        res_grad,
        query_grad,
        out_grad,
    )


def shards(
    llm_hidden,
    slot_start,
    image_group,
    timesteps,
    latents,
    noise,
    kv_weight,
    in_weight,
    res_weight,
    query_weight,
    out_weight,
    cotangent,
):
    own_index = lax.axis_index("img")
    condition = lax.dynamic_slice_in_dim(llm_hidden, slot_start[0], SLOTS, 0)
    kv_part = jnp.dot(condition, kv_weight, preferred_element_type=jnp.float32)
    source_group = lax.dynamic_index_in_dim(image_group, own_index, 0, keepdims=False)
    kv_band = lax.psum_scatter(kv_part, "row", scatter_dimension=0, tiled=True).astype(jnp.bfloat16)
    selected = (image_group == own_index)[:, None, None]
    routed_band = jnp.sum(
        jnp.where(
            selected,
            lax.all_gather(kv_band[None], "img", axis=0, tiled=True).astype(jnp.float32),
            0.0,
        ),
        axis=0,
    ).astype(jnp.bfloat16)
    group_kv = lax.all_gather(routed_band, "row", axis=0, tiled=True)
    noisy = noisy_input(latents[0], noise[0], timesteps[0])
    block_out, grad_kv, res_grad, query_grad, out_grad = block_pass(
        noisy, timesteps[0], group_kv, cotangent[0], in_weight, res_weight, query_weight, out_weight
    )
    grad_band = lax.psum_scatter(
        grad_kv.astype(jnp.bfloat16), "row", scatter_dimension=0, tiled=True
    )
    shard_piece = lax.all_gather(grad_band[None], "img", axis=0, tiled=True)
    indices = jnp.arange(shard_piece.shape[0], dtype=jnp.int32)
    selected = (indices == source_group)[:, None, None]
    routed_grad = jnp.sum(jnp.where(selected, shard_piece.astype(jnp.float32), 0.0), axis=0).astype(
        jnp.bfloat16
    )
    grad_image = lax.all_gather(routed_grad, "row", axis=0, tiled=True)
    grad_condition = lax.dot_general(
        grad_image, kv_weight, (((1,), (1,)), ((), ())), preferred_element_type=jnp.float32
    ).astype(jnp.bfloat16)
    grad_hidden = lax.dynamic_update_slice_in_dim(
        jnp.zeros_like(llm_hidden), grad_condition, slot_start[0], 0
    )
    kv_weight_part = lax.dot_general(
        condition, grad_image, (((0,), (0,)), ((), ())), preferred_element_type=jnp.float32
    )
    kv_weight_total = lax.psum(kv_weight_part.astype(jnp.bfloat16), "img").astype(jnp.float32)
    grad_kv_weight = (kv_weight_total * (lax.axis_size("img") * SLOTS) ** (-0.5)).astype(
        jnp.bfloat16
    )
    weight_scale = (
        lax.axis_size("img") * lax.axis_size("row") * latents.shape[2] * latents.shape[3]
    ) ** (-0.5)
    res_total, query_total, out_total = lax.psum((res_grad, query_grad, out_grad), ("img", "row"))
    grad_res_weight = (res_total * weight_scale).astype(jnp.bfloat16)
    grad_query_weight = (query_total * weight_scale).astype(jnp.bfloat16)
    grad_out_weight = (out_total * weight_scale).astype(jnp.bfloat16)
    return (
        block_out[None],
        grad_hidden,
        grad_kv_weight,
        grad_res_weight,
        grad_query_weight,
        grad_out_weight,
    )


def solution(mesh):
    return jax.shard_map(
        shards,
        mesh=mesh,
        in_specs=(
            P("img", "row"),
            P("img"),
            P(),
            P("img"),
            P("img", None, "row", None),
            P("img", None, "row", None),
            P("row", None),
            P(),
            P(),
            P(),
            P(),
            P("img", None, "row", None),
        ),
        out_specs=(P("img", None, "row", None), P("img", "row"), P("row", None), P(), P(), P()),
        check_vma=False,
    )
```

profile of v0, /device:TPU:0, one launch (start us, length us, event | category | flops | bytes accessed | tf_op | source)
XLA Modules:
  0.0 399.7 jit_solution(4542939119349975653)
XLA Ops:
  8.8 0.6 select_reduce_fusion
  10.8 0.7 add_convert_fusion
  11.6 4.9 %collective-permute-start = (bf16[4,1,128]{2,1,0:T(2,128)(2,1)S(1)}, bf16[4,1,128]{2,1,0:T(2,128)(2,1)S(1)}, u32[]{:S(2)}, u32[]{:S(2)}) collective-permute-start(bf16[4,1,128]{2,1,0:T(2,128)(2,1)S(1)} %get-tuple-element.29), channel_id=1, source_target_pairs={{0,1},{2,3},{4,5},{6,7},{8,9},{10,11},{12,13},{14,15},{16,17},{18,... | collective-permute-start | bytes 3080 | tf_op jit(solution)/shard_map/ppermute | solution.py:19
  16.5 1.3 collective-permute-start.1
  18.5 3.7 fusion.68
  22.3 2.6 convolution_convert_fusion.4
  28.2 0.6 fusion.19
  29.2 4.6 %collective-permute-start.2 = (bf16[320,1,128]{2,1,0:T(2,128)(2,1)S(1)}, bf16[320,1,128]{2,1,0:T(2,128)(2,1)S(1)}, u32[]{:S(2)}, u32[]{:S(2)}) collective-permute-start(bf16[320,1,128]{2,1,0:T(2,128)(2,1)S(1)} %get-tuple-element.17), channel_id=1, source_target_pairs={{0,1},{2,3},{4,5},{6,7},{8,9},{10,11},{12,13},{14,15},{16,17},{18,... | collective-permute-start | bytes 245768 | tf_op jit(solution)/shard_map/ppermute | solution.py:19
  33.8 1.3 collective-permute-start.3
  35.1 1.5 collective-permute-done.2
  36.6 4.4 %collective-permute-done.3 = bf16[320,1,128]{2,1,0:T(2,128)(2,1)S(1)} collective-permute-done((bf16[320,1,128]{2,1,0:T(2,128)(2,1)S(1)}, bf16[320,1,128]{2,1,0:T(2,128)(2,1)S(1)}, u32[]{:S(2)}, u32[]{:S(2)}) %collective-permute-start.3) | collective-permute-done | bytes 81952 | tf_op jit(solution)/shard_map/ppermute | solution.py:21
  41.0 2.7 fusion.6
  43.7 1.3 fusion.146
  45.8 0.6 pad_maximum_fusion
  46.5 0.5 convolution_add_fusion.16
  47.8 0.5 convolution_add_fusion.14
  48.3 0.5 convolution_add_fusion.13
  49.8 0.5 convolution_add_fusion.10
  50.4 0.5 fusion.13
  50.9 0.8 copy-done.1
  51.8 1.3 convolution_convert_fusion.2
  53.1 0.9 convert_element_type.100
  54.0 23.7 %all-gather = bf16[512,640]{1,0:T(8,128)(2,1)S(1)} all-gather(bf16[32,640]{1,0:T(8,128)(2,1)S(1)} %convert_element_type.100), channel_id=2, replica_groups=mesh['img'=16,'row'=2] {'img'}, dimensions={0}, use_global_device_ids=true | all-gather | bytes 696320 | tf_op jit(solution)/shard_map/all_gather | solution.py:190
  77.9 4.7 %all_gather.13 = bf16[64,640]{1,0:T(8,128)(2,1)S(1)} all-gather(bf16[32,640]{1,0:T(8,128)(2,1)S(1)} %fusion.15), channel_id=1, replica_groups=mesh['img'=16,'row'=2] {'row'}, dimensions={0}, use_global_device_ids=true | all-gather | bytes 122880 | tf_op jit(solution)/shard_map/all_gather | solution.py:195
  82.6 0.6 fusion.148
  83.2 0.9 copy.37
  84.1 0.8 copy.26
  84.9 2.7 fusion.150
  87.6 2.0 multiply_reduce_fusion
  90.4 0.6 copy-done.25
  91.2 0.5 fusion.11
  91.8 1.3 fusion.151
  93.1 1.2 convolution_convert_fusion.5
  94.7 0.7 copy-done.30
  95.7 0.7 copy-done.20
  96.5 1.3 fusion.29
  97.8 1.3 fusion.28
  99.1 1.3 fusion.27
  100.5 1.3 fusion.26
  101.8 1.3 fusion.25
  103.1 1.3 fusion.24
  104.4 1.3 fusion.23
  105.7 1.4 fusion.22
  107.1 1.4 fusion.21
  108.4 0.7 pad_maximum_fusion.2
  109.1 1.7 copy.35
  110.9 2.6 convolution_bitcast_fusion.1
  113.6 0.6 dynamic_slice.8
  114.1 0.6 iota_compare_fusion.5
  114.8 2.1 reduce-scatter.7.cloned.1.call-done
  116.9 24.5 %all-gather.1 = bf16[512,640]{1,0:T(8,128)(2,1)S(1)} all-gather(bf16[32,640]{1,0:T(8,128)(2,1)} %reduce-scatter.7.cloned.1.call-done), channel_id=3, replica_groups=mesh['img'=16,'row'=2] {'img'}, dimensions={0}, use_global_device_ids=true | all-gather | bytes 696320 | tf_op jit(solution)/shard_map/all_gather | solution.py:203
  141.6 5.1 %all_gather.15 = bf16[64,640]{1,0:T(8,128)(2,1)S(1)} all-gather(bf16[32,640]{1,0:T(8,128)(2,1)S(1)} %fusion.14), channel_id=1, replica_groups=mesh['img'=16,'row'=2] {'row'}, dimensions={0}, use_global_device_ids=true | all-gather | bytes 122880 | tf_op jit(solution)/shard_map/all_gather | solution.py:209
  146.8 3.4 convolution_convert_fusion
  150.1 1.9 fusion.20
  152.0 1.0 copy.56
  153.0 4.5 %convolution_convert_fusion.1 = bf16[64,3328]{1,0:T(8,128)(2,1)} fusion(bf16[64,640]{1,0:T(8,128)(2,1)S(1)} %all_gather.15, bf16[3328,640]{1,0:T(8,128)(2,1)} %param.18), kind=kOutput, calls=%fused_computation.6 | convolution fusion | flops 272842752 | bytes 4767744 | tf_op jit(solution)/shard_map/dot_general | solution.py:210
  157.5 2.0 broadcast_in_dim.43
  159.4 3.1 dynamic_update_slice.3
  162.5 110.7 %all-reduce.9.cloned.1.call-done = (f32[3,3,320,320]{3,2,1,0:T(8,128)}, f32[320,320]{1,0:T(8,128)}, f32[320,320]{1,0:T(8,128)}) async-done(((f32[3,3,320,320]{3,2,1,0:T(8,128)}, f32[320,320]{1,0:T(8,128)}, f32[320,320]{1,0:T(8,128)}), (f32[3,3,320,320]{3,2,1,0:T(8,128)}, f32[320,320]{1,0:T(8,128)}, f32[320,320]{1,0:T(8,128)})) %all-reduce.9.cloned.1.call-update) | async-done | bytes 4505616 | tf_op jit(solution)/shard_map/psum | solution.py:226
  273.2 1.8 multiply_convert_fusion.3
  274.9 1.8 multiply_convert_fusion.4
  276.7 4.1 %multiply_convert_fusion.1 = bf16[3,3,320,320]{3,2,1,0:T(8,128)(2,1)} fusion(f32[3,3,320,320]{3,2,1,0:T(8,128)} %get-tuple-element.6), kind=kLoop, calls=%fused_computation.7 | loop fusion | flops 1843200 | bytes 5529600 | tf_op jit(solution)/shard_map/convert_element_type | solution.py:227
  280.8 107.4 %all-reduce.7.cloned.1.call-done = bf16[3328,640]{1,0:T(8,128)(2,1)} async-done(((bf16[3328,640]{1,0:T(8,128)(2,1)}), bf16[3328,640]{1,0:T(8,128)(2,1)}) %all-reduce.7.cloned.1.call-update) | async-done | bytes 4259856 | tf_op jit(solution)/shard_map/psum | solution.py:219
  388.1 5.0 %multiply_convert_fusion = bf16[3328,640]{1,0:T(8,128)(2,1)} fusion(bf16[3328,640]{1,0:T(8,128)(2,1)} %all-reduce.7.cloned.1.call-done), kind=kLoop, calls=%fused_computation.1 | loop fusion | flops 6389760 | bytes 8519680 | tf_op jit(solution)/shard_map/convert_element_type | solution.py:220
  (104 shorter events, 9.2 us)
Async XLA Ops:
  7.2 11.3 %copy-start = (bf16[512,3328]{1,0:T(8,128)(2,1)S(1)}, bf16[512,3328]{1,0:T(8,128)(2,1)}, u32[]{:S(2)}) copy-start(bf16[512,3328]{1,0:T(8,128)(2,1)} %param.12) | copy-start | bytes 10223620
  7.2 45.9 %reduce-scatter.5.cloned.1.call-start = ((), (), s32[]{:S(2)}) async-start(), calls=%async_computation.2 | async-start | bytes 245760 | tf_op jit(solution)/shard_map/reduce_scatter | solution.py:185
  11.6 13.4 %collective-permute-start = (bf16[4,1,128]{2,1,0:T(2,128)(2,1)S(1)}, bf16[4,1,128]{2,1,0:T(2,128)(2,1)S(1)}, u32[]{:S(2)}, u32[]{:S(2)}) collective-permute-start(bf16[4,1,128]{2,1,0:T(2,128)(2,1)S(1)} %get-tuple-element.29), channel_id=1, source_target_pairs={{0,1},{2,3},{4,5},{6,7},{8,9},{10,11},{12,13},{14,15},{16,17},{18,... | collective-permute-start | bytes 3080 | tf_op jit(solution)/shard_map/ppermute | solution.py:19
  16.5 8.5 %collective-permute-start.1 = (bf16[4,1,128]{2,1,0:T(2,128)(2,1)S(1)}, bf16[4,1,128]{2,1,0:T(2,128)(2,1)S(1)}, u32[]{:S(2)}, u32[]{:S(2)}) collective-permute-start(bf16[4,1,128]{2,1,0:T(2,128)(2,1)S(1)} %get-tuple-element.30), channel_id=1, source_target_pairs={{1,0},{3,2},{5,4},{7,6},{9,8},{11,10},{13,12},{15,14},{17,16},{19,... | collective-permute-start | bytes 3080 | tf_op jit(solution)/shard_map/ppermute | solution.py:21
  22.2 3.0 copy-start.27
  22.2 94.7 %reduce-scatter.7.cloned.1.call-start = ((), (), s32[]{:S(2)}) async-start(), calls=%async_computation.4 | async-start | bytes 122880 | tf_op jit(solution)/shard_map/reduce_scatter | solution.py:200
  28.8 19.5 %copy-start.3 = (bf16[320,1024]{1,0:T(8,128)(2,1)}, bf16[320,1024]{1,0:T(8,128)(2,1)S(1)}, u32[]{:S(2)}) copy-start(bf16[320,1024]{1,0:T(8,128)(2,1)S(1)} %get-tuple-element.31) | copy-start | bytes 1966084
  28.8 6.2 %copy-start.29 = (s32[16]{0:T(128)S(1)}, s32[16]{0:T(128)}, u32[]{:S(2)}) copy-start(s32[16]{0:T(128)} %param.14) | copy-start | bytes 196
  29.2 7.4 %collective-permute-start.2 = (bf16[320,1,128]{2,1,0:T(2,128)(2,1)S(1)}, bf16[320,1,128]{2,1,0:T(2,128)(2,1)S(1)}, u32[]{:S(2)}, u32[]{:S(2)}) collective-permute-start(bf16[320,1,128]{2,1,0:T(2,128)(2,1)S(1)} %get-tuple-element.17), channel_id=1, source_target_pairs={{0,1},{2,3},{4,5},{6,7},{8,9},{10,11},{12,13},{14,15},{16,17},{18,... | collective-permute-start | bytes 245768 | tf_op jit(solution)/shard_map/ppermute | solution.py:19
  33.8 7.2 %collective-permute-start.3 = (bf16[320,1,128]{2,1,0:T(2,128)(2,1)S(1)}, bf16[320,1,128]{2,1,0:T(2,128)(2,1)S(1)}, u32[]{:S(2)}, u32[]{:S(2)}) collective-permute-start(bf16[320,1,128]{2,1,0:T(2,128)(2,1)S(1)} %get-tuple-element.18), channel_id=1, source_target_pairs={{1,0},{3,2},{5,4},{7,6},{9,8},{11,10},{13,12},{15,14},{17,16},{19,... | collective-permute-start | bytes 245768 | tf_op jit(solution)/shard_map/ppermute | solution.py:21
  43.7 1.6 copy-start.23
  45.0 1.4 copy-start.19
  45.0 2.2 copy-start.17
  45.0 2.7 copy-start.15
  45.1 3.8 copy-start.13
  45.1 4.3 %copy-start.11 = (bf16[320,8,128]{2,1,0:T(8,128)(2,1)}, bf16[320,8,128]{2,1,0:T(8,128)(2,1)S(1)}, u32[]{:S(2)}) copy-start(bf16[320,8,128]{2,1,0:T(8,128)(2,1)S(1)} %get-tuple-element.10) | copy-start | bytes 1966084
  45.1 5.3 %copy-start.21 = (bf16[320,8,128]{2,1,0:T(8,128)(2,1)}, bf16[320,8,128]{2,1,0:T(8,128)(2,1)S(1)}, u32[]{:S(2)}) copy-start(bf16[320,8,128]{2,1,0:T(8,128)(2,1)S(1)} %get-tuple-element.9) | copy-start | bytes 1966084
  46.4 0.8 copy-start.9
  46.5 3.4 copy-start.7
  50.4 1.4 copy-start.24
  50.9 0.8 copy-start.1
  87.6 2.1 copy-start.6
  90.0 0.9 copy-start.25
  90.0 1.2 copy-start.28
  90.3 1.4 copy-start.2
  91.8 1.3 copy-start.26
  93.1 1.2 copy-start.5
  94.3 1.1 copy-start.30
  95.4 1.1 copy-start.20
  96.5 1.3 copy-start.10
  97.8 1.3 copy-start.18
  99.1 1.3 copy-start.16
  100.5 1.3 copy-start.4
  101.8 1.3 copy-start.14
  103.1 1.3 copy-start.12
  104.4 1.3 copy-start.8
  105.7 1.4 copy-start.22
  110.8 162.3 %all-reduce.9.cloned.1.call-start = ((), (), s32[]{:S(2)}) async-start(), calls=%async_computation.5 | async-start | bytes 10813440 | tf_op jit(solution)/shard_map/psum | solution.py:226
  113.5 274.6 %all-reduce.7.cloned.1.call-start = ((), (), s32[]{:S(2)}) async-start(), calls=%async_computation.3 | async-start | bytes 8519680 | tf_op jit(solution)/shard_map/psum | solution.py:219
Sparse Core Ops, SparseCore 0:
  22.3 13.0 reduce-scatter.4
  111.0 5.9 reduce-scatter.6
  123.0 150.1 all-reduce.8
  277.3 110.8 all-reduce.6
where the time goes:
time: 401 us; the launch traced here: 400 us
  waiting for transfers between devices  226 us (56%)
  blocking collectives  58 us (14%)
  matrix products  48.8 us (12%)
  other arithmetic  21 us (5%)
  between operations  17.3 us (4%)
  local copies, waits for them, and re-layouts  16.3 us (4%)
  starting transfers between devices  12.2 us (3%)
    psum x1, waiting for transfers between devices, shards(): lax.psum((res_grad, query_grad, out_grad), ('img', 'row'))  111 us
    psum x1, waiting for transfers between devices, shards(): lax.psum(kv_weight_part.astype(jnp.bfloat16), 'img').astype(jnp.float32)  107 us
    all_gather x1, blocking collectives, shards(): shard_piece = lax.all_gather(grad_band[None], 'img', axis=0, tiled=True)  24.5 us
    all_gather x1, blocking collectives, shards(): lax.all_gather(kv_band[None], 'img', axis=0, tiled=True).astype(jnp.float32)  23.7 us
    dot_general x9, matrix products, filter_grad(): lax.dot_general(upstream, window, (((1,), (1,)), ((), ())), preferred_ele...  11.9 us
    ppermute x2, starting transfers between devices, extended(): lax.ppermute(tail, axis, [(i, (i + 1) % count) for i in range(ends)])  9.45 us
    dot_general x18, matrix products, convolve(): jnp.dot(weight[row_tap, col_tap], window, preferred_element_type=jnp.floa...  8.1 us
  transfers between devices with their start and end apart: 8, of which 5 were waited for; matrix products, arithmetic and copies ran while one was open for 12% of the time, Pallas kernels for 0%

commit v1 on v0

--- a/solution.py
+++ b/solution.py
@@ -223,7 +223,9 @@
     weight_scale = (
         lax.axis_size("img") * lax.axis_size("row") * latents.shape[2] * latents.shape[3]
     ) ** (-0.5)
-    res_total, query_total, out_total = lax.psum((res_grad, query_grad, out_grad), ("img", "row"))
+    res_total, query_total, out_total = lax.psum(
+        lax.psum((res_grad, query_grad, out_grad), "row"), "img"
+    )
     grad_res_weight = (res_total * weight_scale).astype(jnp.bfloat16)
     grad_query_weight = (query_total * weight_scale).astype(jnp.bfloat16)
     grad_out_weight = (out_total * weight_scale).astype(jnp.bfloat16)

time: 401 us -> 514 us (1.28)
  waiting for transfers between devices: 226 us -> 342 us
    psum x1 -> x2, waiting for transfers between devices: 111 us -> 230 us  [the longest x1 125 us: shards(): lax.psum(lax.psum((res_grad, query_grad, out_grad), 'row'), 'img')]
  transfers between devices with their start and end apart: 8 -> 9, of which waited for: 5 -> 6; matrix products, arithmetic and copies ran while one was open for 12% -> 9% of each run, Pallas kernels for 0% -> 0%
where the time goes in v1:
time: 514 us; the launch traced here: 513 us
  waiting for transfers between devices  342 us (67%)
  blocking collectives  57.6 us (11%)
  matrix products  48.6 us (9%)
  other arithmetic  19.1 us (4%)
  between operations  17.3 us (3%)
  local copies, waits for them, and re-layouts  16.3 us (3%)
  starting transfers between devices  12.5 us (2%)
    psum x1, waiting for transfers between devices, shards(): lax.psum(lax.psum((res_grad, query_grad, out_grad), 'row'), 'img')  125 us
    psum x1, waiting for transfers between devices, shards(): lax.psum((res_grad, query_grad, out_grad), 'row')  105 us
    psum x1, waiting for transfers between devices, shards(): lax.psum(kv_weight_part.astype(jnp.bfloat16), 'img').astype(jnp.float32)  104 us
    all_gather x1, blocking collectives, shards(): lax.all_gather(kv_band[None], 'img', axis=0, tiled=True).astype(jnp.float32)  23.6 us
    all_gather x1, blocking collectives, shards(): shard_piece = lax.all_gather(grad_band[None], 'img', axis=0, tiled=True)  23.5 us
    dot_general x9, matrix products, filter_grad(): lax.dot_general(upstream, window, (((1,), (1,)), ((), ())), preferred_ele...  12 us
  transfers between devices with their start and end apart: 9, of which 6 were waited for; matrix products, arithmetic and copies ran while one was open for 9% of the time, Pallas kernels for 0%

profile of v1, /device:TPU:0, one launch (start us, length us, event | category | flops | bytes accessed | tf_op | source)
XLA Modules:
  0.0 513.2 jit_solution(4509876904242219122)
XLA Ops:
  8.8 0.6 select_reduce_fusion
  10.8 0.7 add_convert_fusion
  11.6 4.9 collective-permute-start
  16.5 1.3 collective-permute-start.1
  18.5 3.7 fusion.68
  22.3 2.6 convolution_convert_fusion.4
  28.2 0.6 fusion.19
  29.2 4.6 collective-permute-start.2
  33.8 1.3 collective-permute-start.3
  35.1 1.5 collective-permute-done.2
  36.6 4.4 collective-permute-done.3
  41.0 2.7 fusion.6
  43.7 1.3 fusion.146
  45.8 0.6 pad_maximum_fusion
  46.5 0.5 convolution_add_fusion.16
  47.8 0.5 convolution_add_fusion.14
  49.8 0.5 convolution_add_fusion.10
  50.4 0.5 fusion.13
  50.9 0.8 copy-done.1
  51.8 1.3 convolution_convert_fusion.2
  53.1 0.9 convert_element_type.100
  54.0 23.6 %all-gather = bf16[512,640]{1,0:T(8,128)(2,1)S(1)} all-gather(bf16[32,640]{1,0:T(8,128)(2,1)S(1)} %convert_element_type.100), channel_id=2, replica_groups=mesh['img'=16,'row'=2] {'img'}, dimensions={0}, use_global_device_ids=true | all-gather | bytes 696320 | tf_op jit(solution)/shard_map/all_gather | solution.py:190
  77.8 4.7 all_gather.13
  82.5 0.6 fusion.148
  83.1 0.9 copy.37
  84.0 0.8 copy.26
  84.8 2.7 fusion.150
  87.5 2.0 multiply_reduce_fusion
  90.3 0.6 copy-done.27
  91.2 0.5 fusion.11
  91.7 1.3 fusion.151
  93.1 1.2 convolution_convert_fusion.5
  94.6 0.7 copy-done.32
  95.7 0.7 copy-done.20
  96.4 1.3 fusion.29
  97.7 1.3 fusion.28
  99.1 1.3 fusion.27
  100.4 1.3 fusion.26
  101.7 1.3 fusion.25
  103.1 1.3 fusion.24
  104.4 1.3 fusion.23
  105.7 1.4 fusion.22
  107.0 1.4 fusion.21
  108.4 0.7 pad_maximum_fusion.2
  109.1 1.7 copy.35
  110.8 2.6 convolution_bitcast_fusion.1
  113.5 0.6 dynamic_slice.8
  114.1 0.6 iota_compare_fusion.5
  114.8 2.1 reduce-scatter.7.cloned.1.call-done
  116.9 23.5 %all-gather.1 = bf16[512,640]{1,0:T(8,128)(2,1)S(1)} all-gather(bf16[32,640]{1,0:T(8,128)(2,1)} %reduce-scatter.7.cloned.1.call-done), channel_id=3, replica_groups=mesh['img'=16,'row'=2] {'img'}, dimensions={0}, use_global_device_ids=true | all-gather | bytes 696320 | tf_op jit(solution)/shard_map/all_gather | solution.py:203
  140.5 5.8 %all_gather.15 = bf16[64,640]{1,0:T(8,128)(2,1)S(1)} all-gather(bf16[32,640]{1,0:T(8,128)(2,1)S(1)} %fusion.14), channel_id=1, replica_groups=mesh['img'=16,'row'=2] {'row'}, dimensions={0}, use_global_device_ids=true | all-gather | bytes 122880 | tf_op jit(solution)/shard_map/all_gather | solution.py:209
  146.4 3.4 convolution_convert_fusion
  150.0 105.1 %all-reduce.13.cloned.1.call-done = (f32[3,3,320,320]{3,2,1,0:T(8,128)}, f32[320,320]{1,0:T(8,128)}, f32[320,320]{1,0:T(8,128)}) async-done(((f32[3,3,320,320]{3,2,1,0:T(8,128)}, f32[320,320]{1,0:T(8,128)}, f32[320,320]{1,0:T(8,128)}), (f32[3,3,320,320]{3,2,1,0:T(8,128)}, f32[320,320]{1,0:T(8,128)}, f32[320,320]{1,0:T(8,128)})) %all-reduce.13.cloned.1.call-update) | async-done | bytes 4505616 | tf_op jit(solution)/shard_map/psum | solution.py:227
  255.2 1.9 fusion.20
  257.0 1.0 copy.56
  258.0 4.3 convolution_convert_fusion.1
  262.3 2.0 broadcast_in_dim.43
  264.3 3.1 dynamic_update_slice.3
  267.4 103.7 %all-reduce.9.cloned.1.call-done = bf16[3328,640]{1,0:T(8,128)(2,1)} async-done(((bf16[3328,640]{1,0:T(8,128)(2,1)}), bf16[3328,640]{1,0:T(8,128)(2,1)}) %all-reduce.9.cloned.1.call-update) | async-done | bytes 4259856 | tf_op jit(solution)/shard_map/psum | solution.py:219
  371.1 5.0 multiply_convert_fusion
  376.1 124.9 %all-reduce.11.cloned.1.call-done = (f32[3,3,320,320]{3,2,1,0:T(8,128)}, f32[320,320]{1,0:T(8,128)}, f32[320,320]{1,0:T(8,128)}) async-done(((f32[3,3,320,320]{3,2,1,0:T(8,128)}, f32[320,320]{1,0:T(8,128)}, f32[320,320]{1,0:T(8,128)}), (f32[3,3,320,320]{3,2,1,0:T(8,128)}, f32[320,320]{1,0:T(8,128)}, f32[320,320]{1,0:T(8,128)})) %all-reduce.11.cloned.1.call-update) | async-done | bytes 4505616 | tf_op jit(solution)/shard_map/psum | solution.py:226
  501.0 4.2 multiply_convert_fusion.1
  505.2 0.7 multiply_convert_fusion.3
  505.9 0.7 multiply_convert_fusion.4
  (111 shorter events, 10.0 us)
Async XLA Ops:
  7.2 11.3 %copy-start = (bf16[512,3328]{1,0:T(8,128)(2,1)S(1)}, bf16[512,3328]{1,0:T(8,128)(2,1)}, u32[]{:S(2)}) copy-start(bf16[512,3328]{1,0:T(8,128)(2,1)} %param.12) | copy-start | bytes 10223620
  7.2 45.9 %reduce-scatter.5.cloned.1.call-start = ((), (), s32[]{:S(2)}) async-start(), calls=%async_computation.2 | async-start | bytes 245760 | tf_op jit(solution)/shard_map/reduce_scatter | solution.py:185
  11.6 13.4 %collective-permute-start = (bf16[4,1,128]{2,1,0:T(2,128)(2,1)S(1)}, bf16[4,1,128]{2,1,0:T(2,128)(2,1)S(1)}, u32[]{:S(2)}, u32[]{:S(2)}) collective-permute-start(bf16[4,1,128]{2,1,0:T(2,128)(2,1)S(1)} %get-tuple-element.32), channel_id=1, source_target_pairs={{0,1},{2,3},{4,5},{6,7},{8,9},{10,11},{12,13},{14,15},{16,17},{18,... | collective-permute-start | bytes 3080 | tf_op jit(solution)/shard_map/ppermute | solution.py:19
  16.5 8.5 %collective-permute-start.1 = (bf16[4,1,128]{2,1,0:T(2,128)(2,1)S(1)}, bf16[4,1,128]{2,1,0:T(2,128)(2,1)S(1)}, u32[]{:S(2)}, u32[]{:S(2)}) collective-permute-start(bf16[4,1,128]{2,1,0:T(2,128)(2,1)S(1)} %get-tuple-element.33), channel_id=1, source_target_pairs={{1,0},{3,2},{5,4},{7,6},{9,8},{11,10},{13,12},{15,14},{17,16},{19,... | collective-permute-start | bytes 3080 | tf_op jit(solution)/shard_map/ppermute | solution.py:21
  22.2 3.0 copy-start.29
  22.2 94.7 %reduce-scatter.7.cloned.1.call-start = ((), (), s32[]{:S(2)}) async-start(), calls=%async_computation.4 | async-start | bytes 122880 | tf_op jit(solution)/shard_map/reduce_scatter | solution.py:200
  28.8 19.5 %copy-start.3 = (bf16[320,1024]{1,0:T(8,128)(2,1)}, bf16[320,1024]{1,0:T(8,128)(2,1)S(1)}, u32[]{:S(2)}) copy-start(bf16[320,1024]{1,0:T(8,128)(2,1)S(1)} %get-tuple-element.34) | copy-start | bytes 1966084
  28.8 6.2 %copy-start.31 = (s32[16]{0:T(128)S(1)}, s32[16]{0:T(128)}, u32[]{:S(2)}) copy-start(s32[16]{0:T(128)} %param.14) | copy-start | bytes 196
  29.2 7.4 %collective-permute-start.2 = (bf16[320,1,128]{2,1,0:T(2,128)(2,1)S(1)}, bf16[320,1,128]{2,1,0:T(2,128)(2,1)S(1)}, u32[]{:S(2)}, u32[]{:S(2)}) collective-permute-start(bf16[320,1,128]{2,1,0:T(2,128)(2,1)S(1)} %get-tuple-element.20), channel_id=1, source_target_pairs={{0,1},{2,3},{4,5},{6,7},{8,9},{10,11},{12,13},{14,15},{16,17},{18,... | collective-permute-start | bytes 245768 | tf_op jit(solution)/shard_map/ppermute | solution.py:19
  33.8 7.2 %collective-permute-start.3 = (bf16[320,1,128]{2,1,0:T(2,128)(2,1)S(1)}, bf16[320,1,128]{2,1,0:T(2,128)(2,1)S(1)}, u32[]{:S(2)}, u32[]{:S(2)}) collective-permute-start(bf16[320,1,128]{2,1,0:T(2,128)(2,1)S(1)} %get-tuple-element.21), channel_id=1, source_target_pairs={{1,0},{3,2},{5,4},{7,6},{9,8},{11,10},{13,12},{15,14},{17,16},{19,... | collective-permute-start | bytes 245768 | tf_op jit(solution)/shard_map/ppermute | solution.py:21
  43.7 1.6 copy-start.23
  45.0 1.4 copy-start.19
  45.0 2.2 copy-start.17
  45.0 2.7 copy-start.15
  45.1 3.8 copy-start.13
  45.1 4.3 copy-start.11
  45.1 5.3 %copy-start.21 = (bf16[320,8,128]{2,1,0:T(8,128)(2,1)}, bf16[320,8,128]{2,1,0:T(8,128)(2,1)S(1)}, u32[]{:S(2)}) copy-start(bf16[320,8,128]{2,1,0:T(8,128)(2,1)S(1)} %get-tuple-element.12) | copy-start | bytes 1966084
  46.4 0.8 copy-start.9
  46.5 3.4 copy-start.7
  50.4 1.4 copy-start.26
  50.9 0.8 copy-start.1
  87.5 2.1 copy-start.6
  89.9 0.9 copy-start.27
  90.0 1.2 copy-start.30
  90.3 1.4 copy-start.2
  91.7 1.3 copy-start.28
  93.1 1.2 copy-start.5
  94.2 1.1 copy-start.32
  95.3 1.1 copy-start.20
  96.4 1.3 copy-start.10
  97.7 1.3 copy-start.18
  99.1 1.3 copy-start.16
  100.4 1.3 copy-start.4
  101.7 1.3 copy-start.14
  103.1 1.3 copy-start.12
  104.4 1.3 copy-start.8
  105.7 1.4 copy-start.22
  110.8 144.3 %all-reduce.13.cloned.1.call-start = ((), (), s32[]{:S(2)}) async-start(), calls=%async_computation.6 | async-start | bytes 10813440 | tf_op jit(solution)/shard_map/psum | solution.py:227
  113.5 257.6 %all-reduce.9.cloned.1.call-start = ((), (), s32[]{:S(2)}) async-start(), calls=%async_computation.3 | async-start | bytes 8519680 | tf_op jit(solution)/shard_map/psum | solution.py:219
  149.7 351.3 %all-reduce.11.cloned.1.call-start = ((), (), s32[]{:S(2)}) async-start(), calls=%async_computation.5 | async-start | bytes 10813440 | tf_op jit(solution)/shard_map/psum | solution.py:226
  501.0 4.2 copy-start.25
  501.0 4.9 copy-start.24
Sparse Core Ops, SparseCore 0:
  22.3 13.0 reduce-scatter.4
  110.9 5.9 reduce-scatter.6
  120.1 135.0 all-reduce.12
  259.2 111.7 all-reduce.8
  374.9 126.0 all-reduce.10
